TPU v7x, 128 devices: a whole 4x4x4 slice. The times are simulated.
128 devices in a mesh: ctx: 16 (over z, y), lag: 4 (over x_lo, core), chan: 2 (over x_hi).
Axes of the slice: x: 4 (x_hi: 2, x_lo: 2; x = x_hi * 2 + x_lo), y: 4, z: 4, core: 2. Of those that a mesh axis runs over, the one named last changes fastest.
Arguments:
- values: bfloat16 [2048, 8192], P('ctx', 'chan'), may hold values from -6 to 6
- gate: bfloat16 [2048, 8192], P('ctx', ('chan', 'lag')), may hold values from -6 to 6
- bias: float32 [8192], P('chan'), may hold values from -6 to 6
- filter_taps: bfloat16 [2048, 8192], P('ctx', 'chan'), may hold values from -2 to 2
Outputs:
- mixed: bfloat16 [2048, 8192], P('ctx', ('chan', 'lag'))
All inputs are finite; a program needn't handle non-finite values.
Results may differ from a plain program's by a relative error of at most 0.006.
Values may be sent and summed in bfloat16 or wider, within the bound.
A program may use at most 64 MiB of HBM per device.

v0:
```python
import math

import jax
import jax.numpy as jnp
from jax import lax
from jax.sharding import PartitionSpec as P


def split_table(table):
    upper = table.astype(jnp.bfloat16)
    widened = lax.optimization_barrier(upper).astype(jnp.float32)
    lower = (table - widened).astype(jnp.bfloat16)
    return (upper, lower)


def dft_tables(length, first, count):
    frequency = jnp.arange(length // 2 + 1, dtype=jnp.int32)[:, None]
    item_step_index = first + jnp.arange(count, dtype=jnp.int32)[None, :]
    phase_turns = frequency * item_step_index % length
    phase_angles = phase_turns.astype(jnp.float32) * (2.0 * math.pi / length)
    return (split_table(jnp.cos(phase_angles)), split_table(-jnp.sin(phase_angles)))


def inverse_tables(length, rows):
    row_index = jnp.arange(rows, dtype=jnp.int32)[:, None]
    frequency = jnp.arange(length // 2 + 1, dtype=jnp.int32)[None, :]
    phase_turns = frequency * row_index % length
    phase_angles = phase_turns.astype(jnp.float32) * (2.0 * math.pi / length)
    weights = jnp.where((frequency == 0) | (frequency == length // 2), 1.0, 2.0).astype(jnp.float32)
    return (weights * jnp.cos(phase_angles) / length, -weights * jnp.sin(phase_angles) / length)


def transform(tables, operand):
    cos_parts, sin_parts = tables
    real_part = jnp.einsum(
        "fm,...mc->...fc", cos_parts[0], operand, preferred_element_type=jnp.float32
    )
    real_part = real_part + jnp.einsum(
        "fm,...mc->...fc", cos_parts[1], operand, preferred_element_type=jnp.float32
    )
    imag_part = jnp.einsum(
        "fm,...mc->...fc", sin_parts[0], operand, preferred_element_type=jnp.float32
    )
    imag_part = imag_part + jnp.einsum(
        "fm,...mc->...fc", sin_parts[1], operand, preferred_element_type=jnp.float32
    )
    return (real_part, imag_part)


def spectrum_pair(low_tables, high_tables, current, previous):
    first_re, first_im = transform(low_tables, current)
    second_re, second_im = transform(high_tables, previous)
    return (first_re + second_re, first_im + second_im)


def inverse(back_cos, back_sin, total_re, total_im):
    result = jnp.einsum("rf,...fc->...rc", back_cos, total_re, preferred_element_type=jnp.float32)
    return result + jnp.einsum(
        "rf,...fc->...rc", back_sin, total_im, preferred_element_type=jnp.float32
    )


def body(values, gate, bias, filter_taps):
    tok_rows = values.shape[0]
    length = 2 * tok_rows
    lag_count = lax.axis_size("lag")
    lag_index = lax.axis_index("lag")
    low_tables = dft_tables(length, 0, tok_rows)
    high_tables = dft_tables(length, tok_rows, tok_rows)
    back_cos, back_sin = inverse_tables(length, tok_rows)
    share_width = values.shape[1] // lag_count
    value_share = lax.dynamic_slice_in_dim(values, lag_index * share_width, share_width, 1)
    taps_share = lax.dynamic_slice_in_dim(filter_taps, lag_index * share_width, share_width, 1)
    cols_values, cols_taps = (
        lax.all_to_all(value_share, "ctx", split_axis=1, concat_axis=0, tiled=True),
        lax.all_to_all(taps_share, "ctx", split_axis=1, concat_axis=0, tiled=True),
    )
    block_count = lax.axis_size("ctx")
    narrow = cols_values.shape[1]
    value_blocks = cols_values.reshape(block_count, tok_rows, narrow)
    taps_blocks = cols_taps.reshape(block_count, tok_rows, narrow)
    earlier = jnp.concatenate([jnp.zeros_like(taps_blocks[:1]), taps_blocks[:-1]], axis=0)
    kernel_real_entry, filt_im = spectrum_pair(low_tables, high_tables, taps_blocks, earlier)
    val_re, val_im = transform(low_tables, value_blocks)
    padded_re = jnp.concatenate([jnp.zeros_like(val_re), val_re], axis=0)
    padded_im = jnp.concatenate([jnp.zeros_like(val_im), val_im], axis=0)

    def add_lag(lag_step, carry):
        acc_re, acc_im = carry
        start = (block_count - lag_step).astype(jnp.int32)
        moved_re = lax.dynamic_slice_in_dim(padded_re, start, block_count, 0)
        moved_im = lax.dynamic_slice_in_dim(padded_im, start, block_count, 0)
        coef_re = lax.dynamic_index_in_dim(kernel_real_entry, lag_step, 0, keepdims=True)
        coef_im = lax.dynamic_index_in_dim(filt_im, lag_step, 0, keepdims=True)
        acc_re = acc_re + coef_re * moved_re - coef_im * moved_im
        acc_im = acc_im + coef_re * moved_im + coef_im * moved_re
        return (acc_re, acc_im)

    empty = jnp.zeros(val_re.shape, jnp.float32)
    total_re, total_im = lax.fori_loop(0, block_count, add_lag, (empty, empty))
    convolved = inverse(back_cos, back_sin, total_re, total_im).reshape(
        block_count * tok_rows, narrow
    )
    ctx_index = lax.axis_index("ctx")
    own_bias = lax.dynamic_slice_in_dim(
        bias, lag_index * share_width + ctx_index * narrow, narrow, 0
    )
    before_gate = convolved + own_bias[None, :] * cols_values.astype(jnp.float32)
    returned = lax.all_to_all(before_gate, "ctx", split_axis=0, concat_axis=1, tiled=True)
    mixed = gate.astype(jnp.float32) * returned
    return mixed.astype(jnp.bfloat16)


def solution(mesh):
    return jax.shard_map(
        body,
        mesh=mesh,
        in_specs=(P("ctx", "chan"), P("ctx", ("chan", "lag")), P("chan"), P("ctx", "chan")),
        out_specs=P("ctx", ("chan", "lag")),
        check_vma=False,
    )
```

profile of v0, /device:TPU:0, one launch (start us, length us, event | category | flops | bytes accessed | tf_op | source)
XLA Modules:
  0.0 169.9 jit_solution(2524083890596160496)
XLA Ops:
  1.9 8.2 %all-to-all-start = ((bf16[128,16,64]{0,2,1:T(8,128)(2,1)}), bf16[128,16,64]{0,2,1:T(8,128)(2,1)S(1)}, u32[]{:S(2)}, u32[]{:S(2)}) async-start(bf16[128,16,64]{0,2,1:T(8,128)(2,1)} %bitcast), calls=%async_computation | async-start | bytes 524288 | tf_op jit(solution)/shard_map/all_to_all | solution.py:76
  12.6 6.2 %all-to-all-done = bf16[128,16,64]{0,2,1:T(8,128)(2,1)S(1)} async-done(((bf16[128,16,64]{0,2,1:T(8,128)(2,1)}), bf16[128,16,64]{0,2,1:T(8,128)(2,1)S(1)}, u32[]{:S(2)}, u32[]{:S(2)}) %all-to-all-start) | async-done | bytes 262176 | tf_op jit(solution)/shard_map/all_to_all | solution.py:76
  18.8 3.5 %all-to-all-start.1 = ((bf16[128,16,64]{0,2,1:T(8,128)(2,1)}), bf16[128,16,64]{0,2,1:T(8,128)(2,1)S(1)}, u32[]{:S(2)}, u32[]{:S(2)}) async-start(bf16[128,16,64]{0,2,1:T(8,128)(2,1)} %bitcast.7), calls=%async_computation.1 | async-start | bytes 524288 | tf_op jit(solution)/shard_map/all_to_all | solution.py:75
  23.4 7.6 %all-to-all-done.1 = bf16[128,16,64]{0,2,1:T(8,128)(2,1)S(1)} async-done(((bf16[128,16,64]{0,2,1:T(8,128)(2,1)}), bf16[128,16,64]{0,2,1:T(8,128)(2,1)S(1)}, u32[]{:S(2)}, u32[]{:S(2)}) %all-to-all-start.1) | async-done | bytes 262176 | tf_op jit(solution)/shard_map/all_to_all | solution.py:75
  41.6 111.6 %while.18 = (s32[]{:T(128)}, f32[16,129,64]{2,1,0:T(8,128)}, f32[16,129,64]{2,1,0:T(8,128)}, f32[16,129,64]{1,2,0:T(8,128)}, f32[32,129,64]{1,2,0:T(8,128)}, /*i...) while((s32[]{:T(128)}, f32[16,129,64]{2,1,0:T(8,128)}, ...), condition=%wide.region_1.2_spmd.clone, body=%wide.region_0.1_spmd.clone.sunk | while | flops 1320967 | bytes 7727789 | solution.py:100
  41.6 1.7 %constant_dynamic-slice_fusion.8 = (f32[16,129,64]{1,2,0:T(8,128)S(1)}, f32[16,129,64]{1,2,0:T(8,128)S(1)}) fusion(f32[32,129,64]{1,2,0:T(8,128)} %get-tuple-element.322, s32[]{:T(128)S(6)} %select_n.161, f32[32,129,64]{1,2,0:T(8,128)} %get-tuple-element.320), kind=kLoop, calls=%fused_computation.4.clone.1 | loop fusion | bytes 2113540 | tf_op jit(solution)/shard_map/while/body/eval_jaxpr/dynamic_slice | solution.py:92
  45.3 1.7 %fusion.153 = (f32[16,129,64]{2,1,0:T(8,128)}, f32[16,129,64]{2,1,0:T(8,128)}) fusion(f32[16,129,64]{2,1,0:T(8,128)} %get-tuple-element.307, f32[16,129,64]{2,1,0:T(8,128)S(1)} %copy.24, f32[16,129,64]{2,1,0:T(8,128)S(1)} %copy.25, f32[129,64]{1,0:T(8,128)S(1)} %bitcast.84, f32[129,64]{1,0:T(8,128)S(1)} %bitcast.85, pred[]{:T(512)S(6)} %compare.9, ...), kind=kLoop, calls=%fused_computation.1.clone.1 | loop fusion | flops 1320960 | bytes 3236353 | tf_op jit(solution)/shard_map/while/body/eval_jaxpr/add | solution.py:96
  47.1 1.7 %constant_dynamic-slice_fusion.8 = (f32[16,129,64]{1,2,0:T(8,128)S(1)}, f32[16,129,64]{1,2,0:T(8,128)S(1)}) fusion(f32[32,129,64]{1,2,0:T(8,128)} %get-tuple-element.322, s32[]{:T(128)S(6)} %select_n.161, f32[32,129,64]{1,2,0:T(8,128)} %get-tuple-element.320), kind=kLoop, calls=%fused_computation.4.clone.1 | loop fusion | bytes 2113540 | tf_op jit(solution)/shard_map/while/body/eval_jaxpr/dynamic_slice | solution.py:92
  50.8 3.3 %fusion.153 = (f32[16,129,64]{2,1,0:T(8,128)}, f32[16,129,64]{2,1,0:T(8,128)}) fusion(f32[16,129,64]{2,1,0:T(8,128)} %get-tuple-element.307, f32[16,129,64]{2,1,0:T(8,128)S(1)} %copy.24, f32[16,129,64]{2,1,0:T(8,128)S(1)} %copy.25, f32[129,64]{1,0:T(8,128)S(1)} %bitcast.84, f32[129,64]{1,0:T(8,128)S(1)} %bitcast.85, pred[]{:T(512)S(6)} %compare.9, ...), kind=kLoop, calls=%fused_computation.1.clone.1 | loop fusion | flops 1320960 | bytes 3236353 | tf_op jit(solution)/shard_map/while/body/eval_jaxpr/add | solution.py:96
  54.1 1.7 %constant_dynamic-slice_fusion.8 = (f32[16,129,64]{1,2,0:T(8,128)S(1)}, f32[16,129,64]{1,2,0:T(8,128)S(1)}) fusion(f32[32,129,64]{1,2,0:T(8,128)} %get-tuple-element.322, s32[]{:T(128)S(6)} %select_n.161, f32[32,129,64]{1,2,0:T(8,128)} %get-tuple-element.320), kind=kLoop, calls=%fused_computation.4.clone.1 | loop fusion | bytes 2113540 | tf_op jit(solution)/shard_map/while/body/eval_jaxpr/dynamic_slice | solution.py:92
  57.9 3.3 %fusion.153 = (f32[16,129,64]{2,1,0:T(8,128)}, f32[16,129,64]{2,1,0:T(8,128)}) fusion(f32[16,129,64]{2,1,0:T(8,128)} %get-tuple-element.307, f32[16,129,64]{2,1,0:T(8,128)S(1)} %copy.24, f32[16,129,64]{2,1,0:T(8,128)S(1)} %copy.25, f32[129,64]{1,0:T(8,128)S(1)} %bitcast.84, f32[129,64]{1,0:T(8,128)S(1)} %bitcast.85, pred[]{:T(512)S(6)} %compare.9, ...), kind=kLoop, calls=%fused_computation.1.clone.1 | loop fusion | flops 1320960 | bytes 3236353 | tf_op jit(solution)/shard_map/while/body/eval_jaxpr/add | solution.py:96
  61.2 1.7 %constant_dynamic-slice_fusion.8 = (f32[16,129,64]{1,2,0:T(8,128)S(1)}, f32[16,129,64]{1,2,0:T(8,128)S(1)}) fusion(f32[32,129,64]{1,2,0:T(8,128)} %get-tuple-element.322, s32[]{:T(128)S(6)} %select_n.161, f32[32,129,64]{1,2,0:T(8,128)} %get-tuple-element.320), kind=kLoop, calls=%fused_computation.4.clone.1 | loop fusion | bytes 2113540 | tf_op jit(solution)/shard_map/while/body/eval_jaxpr/dynamic_slice | solution.py:92
  65.0 3.3 %fusion.153 = (f32[16,129,64]{2,1,0:T(8,128)}, f32[16,129,64]{2,1,0:T(8,128)}) fusion(f32[16,129,64]{2,1,0:T(8,128)} %get-tuple-element.307, f32[16,129,64]{2,1,0:T(8,128)S(1)} %copy.24, f32[16,129,64]{2,1,0:T(8,128)S(1)} %copy.25, f32[129,64]{1,0:T(8,128)S(1)} %bitcast.84, f32[129,64]{1,0:T(8,128)S(1)} %bitcast.85, pred[]{:T(512)S(6)} %compare.9, ...), kind=kLoop, calls=%fused_computation.1.clone.1 | loop fusion | flops 1320960 | bytes 3236353 | tf_op jit(solution)/shard_map/while/body/eval_jaxpr/add | solution.py:96
  68.3 1.7 %constant_dynamic-slice_fusion.8 = (f32[16,129,64]{1,2,0:T(8,128)S(1)}, f32[16,129,64]{1,2,0:T(8,128)S(1)}) fusion(f32[32,129,64]{1,2,0:T(8,128)} %get-tuple-element.322, s32[]{:T(128)S(6)} %select_n.161, f32[32,129,64]{1,2,0:T(8,128)} %get-tuple-element.320), kind=kLoop, calls=%fused_computation.4.clone.1 | loop fusion | bytes 2113540 | tf_op jit(solution)/shard_map/while/body/eval_jaxpr/dynamic_slice | solution.py:92
  72.0 3.3 %fusion.153 = (f32[16,129,64]{2,1,0:T(8,128)}, f32[16,129,64]{2,1,0:T(8,128)}) fusion(f32[16,129,64]{2,1,0:T(8,128)} %get-tuple-element.307, f32[16,129,64]{2,1,0:T(8,128)S(1)} %copy.24, f32[16,129,64]{2,1,0:T(8,128)S(1)} %copy.25, f32[129,64]{1,0:T(8,128)S(1)} %bitcast.84, f32[129,64]{1,0:T(8,128)S(1)} %bitcast.85, pred[]{:T(512)S(6)} %compare.9, ...), kind=kLoop, calls=%fused_computation.1.clone.1 | loop fusion | flops 1320960 | bytes 3236353 | tf_op jit(solution)/shard_map/while/body/eval_jaxpr/add | solution.py:96
  79.1 3.3 %fusion.153 = (f32[16,129,64]{2,1,0:T(8,128)}, f32[16,129,64]{2,1,0:T(8,128)}) fusion(f32[16,129,64]{2,1,0:T(8,128)} %get-tuple-element.307, f32[16,129,64]{2,1,0:T(8,128)S(1)} %copy.24, f32[16,129,64]{2,1,0:T(8,128)S(1)} %copy.25, f32[129,64]{1,0:T(8,128)S(1)} %bitcast.84, f32[129,64]{1,0:T(8,128)S(1)} %bitcast.85, pred[]{:T(512)S(6)} %compare.9, ...), kind=kLoop, calls=%fused_computation.1.clone.1 | loop fusion | flops 1320960 | bytes 3236353 | tf_op jit(solution)/shard_map/while/body/eval_jaxpr/add | solution.py:96
  82.4 1.7 %constant_dynamic-slice_fusion.8 = (f32[16,129,64]{1,2,0:T(8,128)S(1)}, f32[16,129,64]{1,2,0:T(8,128)S(1)}) fusion(f32[32,129,64]{1,2,0:T(8,128)} %get-tuple-element.322, s32[]{:T(128)S(6)} %select_n.161, f32[32,129,64]{1,2,0:T(8,128)} %get-tuple-element.320), kind=kLoop, calls=%fused_computation.4.clone.1 | loop fusion | bytes 2113540 | tf_op jit(solution)/shard_map/while/body/eval_jaxpr/dynamic_slice | solution.py:92
  86.2 3.3 %fusion.153 = (f32[16,129,64]{2,1,0:T(8,128)}, f32[16,129,64]{2,1,0:T(8,128)}) fusion(f32[16,129,64]{2,1,0:T(8,128)} %get-tuple-element.307, f32[16,129,64]{2,1,0:T(8,128)S(1)} %copy.24, f32[16,129,64]{2,1,0:T(8,128)S(1)} %copy.25, f32[129,64]{1,0:T(8,128)S(1)} %bitcast.84, f32[129,64]{1,0:T(8,128)S(1)} %bitcast.85, pred[]{:T(512)S(6)} %compare.9, ...), kind=kLoop, calls=%fused_computation.1.clone.1 | loop fusion | flops 1320960 | bytes 3236353 | tf_op jit(solution)/shard_map/while/body/eval_jaxpr/add | solution.py:96
  89.5 1.7 %constant_dynamic-slice_fusion.8 = (f32[16,129,64]{1,2,0:T(8,128)S(1)}, f32[16,129,64]{1,2,0:T(8,128)S(1)}) fusion(f32[32,129,64]{1,2,0:T(8,128)} %get-tuple-element.322, s32[]{:T(128)S(6)} %select_n.161, f32[32,129,64]{1,2,0:T(8,128)} %get-tuple-element.320), kind=kLoop, calls=%fused_computation.4.clone.1 | loop fusion | bytes 2113540 | tf_op jit(solution)/shard_map/while/body/eval_jaxpr/dynamic_slice | solution.py:92
  93.3 3.3 %fusion.153 = (f32[16,129,64]{2,1,0:T(8,128)}, f32[16,129,64]{2,1,0:T(8,128)}) fusion(f32[16,129,64]{2,1,0:T(8,128)} %get-tuple-element.307, f32[16,129,64]{2,1,0:T(8,128)S(1)} %copy.24, f32[16,129,64]{2,1,0:T(8,128)S(1)} %copy.25, f32[129,64]{1,0:T(8,128)S(1)} %bitcast.84, f32[129,64]{1,0:T(8,128)S(1)} %bitcast.85, pred[]{:T(512)S(6)} %compare.9, ...), kind=kLoop, calls=%fused_computation.1.clone.1 | loop fusion | flops 1320960 | bytes 3236353 | tf_op jit(solution)/shard_map/while/body/eval_jaxpr/add | solution.py:96
  100.3 3.3 %fusion.153 = (f32[16,129,64]{2,1,0:T(8,128)}, f32[16,129,64]{2,1,0:T(8,128)}) fusion(f32[16,129,64]{2,1,0:T(8,128)} %get-tuple-element.307, f32[16,129,64]{2,1,0:T(8,128)S(1)} %copy.24, f32[16,129,64]{2,1,0:T(8,128)S(1)} %copy.25, f32[129,64]{1,0:T(8,128)S(1)} %bitcast.84, f32[129,64]{1,0:T(8,128)S(1)} %bitcast.85, pred[]{:T(512)S(6)} %compare.9, ...), kind=kLoop, calls=%fused_computation.1.clone.1 | loop fusion | flops 1320960 | bytes 3236353 | tf_op jit(solution)/shard_map/while/body/eval_jaxpr/add | solution.py:96
  107.4 3.3 %fusion.153 = (f32[16,129,64]{2,1,0:T(8,128)}, f32[16,129,64]{2,1,0:T(8,128)}) fusion(f32[16,129,64]{2,1,0:T(8,128)} %get-tuple-element.307, f32[16,129,64]{2,1,0:T(8,128)S(1)} %copy.24, f32[16,129,64]{2,1,0:T(8,128)S(1)} %copy.25, f32[129,64]{1,0:T(8,128)S(1)} %bitcast.84, f32[129,64]{1,0:T(8,128)S(1)} %bitcast.85, pred[]{:T(512)S(6)} %compare.9, ...), kind=kLoop, calls=%fused_computation.1.clone.1 | loop fusion | flops 1320960 | bytes 3236353 | tf_op jit(solution)/shard_map/while/body/eval_jaxpr/add | solution.py:96
  114.5 3.3 %fusion.153 = (f32[16,129,64]{2,1,0:T(8,128)}, f32[16,129,64]{2,1,0:T(8,128)}) fusion(f32[16,129,64]{2,1,0:T(8,128)} %get-tuple-element.307, f32[16,129,64]{2,1,0:T(8,128)S(1)} %copy.24, f32[16,129,64]{2,1,0:T(8,128)S(1)} %copy.25, f32[129,64]{1,0:T(8,128)S(1)} %bitcast.84, f32[129,64]{1,0:T(8,128)S(1)} %bitcast.85, pred[]{:T(512)S(6)} %compare.9, ...), kind=kLoop, calls=%fused_computation.1.clone.1 | loop fusion | flops 1320960 | bytes 3236353 | tf_op jit(solution)/shard_map/while/body/eval_jaxpr/add | solution.py:96
  121.6 3.3 %fusion.153 = (f32[16,129,64]{2,1,0:T(8,128)}, f32[16,129,64]{2,1,0:T(8,128)}) fusion(f32[16,129,64]{2,1,0:T(8,128)} %get-tuple-element.307, f32[16,129,64]{2,1,0:T(8,128)S(1)} %copy.24, f32[16,129,64]{2,1,0:T(8,128)S(1)} %copy.25, f32[129,64]{1,0:T(8,128)S(1)} %bitcast.84, f32[129,64]{1,0:T(8,128)S(1)} %bitcast.85, pred[]{:T(512)S(6)} %compare.9, ...), kind=kLoop, calls=%fused_computation.1.clone.1 | loop fusion | flops 1320960 | bytes 3236353 | tf_op jit(solution)/shard_map/while/body/eval_jaxpr/add | solution.py:96
  124.9 1.7 %constant_dynamic-slice_fusion.8 = (f32[16,129,64]{1,2,0:T(8,128)S(1)}, f32[16,129,64]{1,2,0:T(8,128)S(1)}) fusion(f32[32,129,64]{1,2,0:T(8,128)} %get-tuple-element.322, s32[]{:T(128)S(6)} %select_n.161, f32[32,129,64]{1,2,0:T(8,128)} %get-tuple-element.320), kind=kLoop, calls=%fused_computation.4.clone.1 | loop fusion | bytes 2113540 | tf_op jit(solution)/shard_map/while/body/eval_jaxpr/dynamic_slice | solution.py:92
  128.6 3.3 %fusion.153 = (f32[16,129,64]{2,1,0:T(8,128)}, f32[16,129,64]{2,1,0:T(8,128)}) fusion(f32[16,129,64]{2,1,0:T(8,128)} %get-tuple-element.307, f32[16,129,64]{2,1,0:T(8,128)S(1)} %copy.24, f32[16,129,64]{2,1,0:T(8,128)S(1)} %copy.25, f32[129,64]{1,0:T(8,128)S(1)} %bitcast.84, f32[129,64]{1,0:T(8,128)S(1)} %bitcast.85, pred[]{:T(512)S(6)} %compare.9, ...), kind=kLoop, calls=%fused_computation.1.clone.1 | loop fusion | flops 1320960 | bytes 3236353 | tf_op jit(solution)/shard_map/while/body/eval_jaxpr/add | solution.py:96
  132.0 1.7 %constant_dynamic-slice_fusion.8 = (f32[16,129,64]{1,2,0:T(8,128)S(1)}, f32[16,129,64]{1,2,0:T(8,128)S(1)}) fusion(f32[32,129,64]{1,2,0:T(8,128)} %get-tuple-element.322, s32[]{:T(128)S(6)} %select_n.161, f32[32,129,64]{1,2,0:T(8,128)} %get-tuple-element.320), kind=kLoop, calls=%fused_computation.4.clone.1 | loop fusion | bytes 2113540 | tf_op jit(solution)/shard_map/while/body/eval_jaxpr/dynamic_slice | solution.py:92
  135.7 3.3 %fusion.153 = (f32[16,129,64]{2,1,0:T(8,128)}, f32[16,129,64]{2,1,0:T(8,128)}) fusion(f32[16,129,64]{2,1,0:T(8,128)} %get-tuple-element.307, f32[16,129,64]{2,1,0:T(8,128)S(1)} %copy.24, f32[16,129,64]{2,1,0:T(8,128)S(1)} %copy.25, f32[129,64]{1,0:T(8,128)S(1)} %bitcast.84, f32[129,64]{1,0:T(8,128)S(1)} %bitcast.85, pred[]{:T(512)S(6)} %compare.9, ...), kind=kLoop, calls=%fused_computation.1.clone.1 | loop fusion | flops 1320960 | bytes 3236353 | tf_op jit(solution)/shard_map/while/body/eval_jaxpr/add | solution.py:96
  142.8 3.3 %fusion.153 = (f32[16,129,64]{2,1,0:T(8,128)}, f32[16,129,64]{2,1,0:T(8,128)}) fusion(f32[16,129,64]{2,1,0:T(8,128)} %get-tuple-element.307, f32[16,129,64]{2,1,0:T(8,128)S(1)} %copy.24, f32[16,129,64]{2,1,0:T(8,128)S(1)} %copy.25, f32[129,64]{1,0:T(8,128)S(1)} %bitcast.84, f32[129,64]{1,0:T(8,128)S(1)} %bitcast.85, pred[]{:T(512)S(6)} %compare.9, ...), kind=kLoop, calls=%fused_computation.1.clone.1 | loop fusion | flops 1320960 | bytes 3236353 | tf_op jit(solution)/shard_map/while/body/eval_jaxpr/add | solution.py:96
  149.9 3.3 %fusion.153 = (f32[16,129,64]{2,1,0:T(8,128)}, f32[16,129,64]{2,1,0:T(8,128)}) fusion(f32[16,129,64]{2,1,0:T(8,128)} %get-tuple-element.307, f32[16,129,64]{2,1,0:T(8,128)S(1)} %copy.24, f32[16,129,64]{2,1,0:T(8,128)S(1)} %copy.25, f32[129,64]{1,0:T(8,128)S(1)} %bitcast.84, f32[129,64]{1,0:T(8,128)S(1)} %bitcast.85, pred[]{:T(512)S(6)} %compare.9, ...), kind=kLoop, calls=%fused_computation.1.clone.1 | loop fusion | flops 1320960 | bytes 3236353 | tf_op jit(solution)/shard_map/while/body/eval_jaxpr/add | solution.py:96
  153.2 1.9 %fusion.32 = f32[16,64,128]{2,1,0:T(8,128)S(1)} fusion(f32[16,129,64]{2,1,0:T(8,128)} %get-tuple-element.182, f32[129]{0:T(256)S(1)} %or_select_fusion), kind=kOutput, calls=%fused_computation.55 | convolution fusion | flops 34080768 | bytes 1053188 | tf_op jit(solution)/shard_map/rf,...fc->...rc/dot_general | solution.py:57
  155.7 13.2 %all_to_all.48 = f32[16,128,64]{1,2,0:T(8,128)S(1)} all-to-all(f32[16,128,64]{1,2,0:T(8,128)S(1)} %fusion.9), channel_id=1, replica_groups=mesh['ctx'=16,'lag'=4,'chan'=2] {'ctx'}, dimensions={0} | all-to-all | bytes 1048576 | tf_op jit(solution)/shard_map/all_to_all | solution.py:109
  (120 shorter events, 62.0 us)
Async XLA Ops:
  1.9 16.9 %all-to-all-start = ((bf16[128,16,64]{0,2,1:T(8,128)(2,1)}), bf16[128,16,64]{0,2,1:T(8,128)(2,1)S(1)}, u32[]{:S(2)}, u32[]{:S(2)}) async-start(bf16[128,16,64]{0,2,1:T(8,128)(2,1)} %bitcast), calls=%async_computation | async-start | bytes 524288 | tf_op jit(solution)/shard_map/all_to_all | solution.py:76
  18.8 12.2 %all-to-all-start.1 = ((bf16[128,16,64]{0,2,1:T(8,128)(2,1)}), bf16[128,16,64]{0,2,1:T(8,128)(2,1)S(1)}, u32[]{:S(2)}, u32[]{:S(2)}) async-start(bf16[128,16,64]{0,2,1:T(8,128)(2,1)} %bitcast.7), calls=%async_computation.1 | async-start | bytes 524288 | tf_op jit(solution)/shard_map/all_to_all | solution.py:75
  153.2 1.9 %copy-start = (f32[16,129,64]{2,1,0:T(8,128)S(1)}, f32[16,129,64]{2,1,0:T(8,128)}, u32[]{:S(2)}) copy-start(f32[16,129,64]{2,1,0:T(8,128)} %get-tuple-element.183) | copy-start | bytes 1585156
  155.7 13.4 %copy-start.1 = (bf16[128,1024]{1,0:T(8,128)(2,1)S(1)}, bf16[128,1024]{1,0:T(8,128)(2,1)}, u32[]{:S(2)}) copy-start(bf16[128,1024]{1,0:T(8,128)(2,1)} %param.7) | copy-start | bytes 786436
where the time goes:
time: 172 us; the launch traced here: 170 us
  local copies, waits for them, and re-layouts  66.5 us (39%)
  other arithmetic  53.1 us (31%)
  waiting for transfers between devices  13.7 us (8%)
  blocking collectives  13.2 us (8%)
  starting transfers between devices  11.7 us (7%)
  matrix products  11.1 us (6%)
    add x16, other arithmetic, add_lag(): acc_im = acc_im + coef_re * moved_im + coef_im * moved_re  51.5 us
    dynamic_slice x32, local copies, waits for them, and re-layouts, add_lag(): moved_im = lax.dynamic_slice_in_dim(padded_im, start, block_count, 0)  34.9 us
    dynamic_slice x32, local copies, waits for them, and re-layouts, add_lag(): coef_im = lax.dynamic_index_in_dim(filt_im, lag_step, 0, keepdims=True)  15.7 us
    all_to_all x1, blocking collectives, body(): lax.all_to_all(before_gate, 'ctx', split_axis=0, concat_axis=1, tiled=True)  13.2 us
    all_to_all x1, starting transfers between devices, body(): lax.all_to_all(taps_share, 'ctx', split_axis=1, concat_axis=0, tiled=True)  8.16 us
    dynamic_slice x16, local copies, waits for them, and re-layouts, add_lag(): moved_re = lax.dynamic_slice_in_dim(padded_re, start, block_count, 0)  7.61 us
    all_to_all x1, waiting for transfers between devices, body(): lax.all_to_all(value_share, 'ctx', split_axis=1, concat_axis=0, tiled=True)  7.58 us
    all_to_all x1, waiting for transfers between devices, body(): lax.all_to_all(taps_share, 'ctx', split_axis=1, concat_axis=0, tiled=True)  6.17 us
  transfers between devices with their start and end apart: 2, of which 2 were waited for; matrix products, arithmetic and copies ran while one was open for 2% of the time, Pallas kernels for 0%

commit v1 on v0

v1 whole, which is shorter than its diff:
```python
import functools
import math

import jax
import jax.numpy as jnp
import numpy as np
from jax import lax
from jax.experimental import pallas as pl
from jax.experimental.pallas import tpu as pltpu
from jax.sharding import PartitionSpec as P

MESH = pl.DeviceIdType.MESH
LANES = 128
HALF = 64
SIDE = 4


def halves(table):
    upper = table.astype(jnp.bfloat16)
    lower = (table - upper.astype(np.float64)).astype(jnp.bfloat16)
    return upper, lower


def tables(rows):
    length = 2 * rows
    order = np.arange(rows)
    freq = np.where(order < rows // 2, 2 * order, 2 * (order - rows // 2) + 1)
    token = np.arange(rows)
    angle = 2.0 * math.pi * ((freq[:, None] * token[None, :]) % length) / length
    alternate = np.where(token % 2 == 0, 1.0, -1.0)
    real, imag = np.cos(angle), -np.sin(angle)
    imag[0] = alternate
    weight = np.where(order == 0, 1.0, 2.0) / length
    back_real = (real * weight[:, None]).T
    back_imag = (imag * weight[:, None]).T
    back_imag[:, 0] = -alternate / length
    forward = np.concatenate([real, imag], axis=0)
    backward = np.concatenate([back_real, back_imag], axis=1)
    return halves(forward), halves(backward)


def hops(offset):
    return sum(min(part, SIDE - part) for part in divmod(offset, SIDE))


def peer_of(me, offset, count):
    dz, dy = divmod(offset, SIDE)
    z, y = me // SIDE, me % SIDE
    return ((z + dz) % (count // SIDE)) * SIDE + (y + dy) % SIDE


def kernel(
    count,
    values_hbm,
    taps_hbm,
    gate_hbm,
    bias_hbm,
    fwd_hi_hbm,
    fwd_lo_hbm,
    inv_hi_hbm,
    inv_lo_hbm,
    out_ref,
    vbuf,
    tbuf,
    gbuf,
    bbuf,
    fwd_hi,
    fwd_lo,
    inv_hi,
    inv_lo,
    packed,
    blocks,
    spec_a,
    sum_a,
    spec_b,
    sum_b,
    total,
    ret_send,
    ret_recv,
    load_sem,
    send_sem,
    recv_sem,
    back_send_sem,
    back_recv_sem,
):
    me = lax.axis_index("ctx")
    lag = lax.axis_index("lag")
    rows = vbuf.shape[0]
    share = vbuf.shape[1]
    tiles = share // LANES
    offsets = sorted(range(1, count), key=lambda o: -hops(o))

    barrier = pltpu.get_barrier_semaphore()
    for offset in offsets:
        pl.semaphore_signal(
            barrier, inc=1, device_id={"ctx": peer_of(me, offset, count)}, device_id_type=MESH
        )

    columns = pl.ds(pl.multiple_of(lag * share, share), share)
    loads = [
        pltpu.make_async_copy(src, dst, load_sem.at[i])
        for i, (src, dst) in enumerate(
            [
                (taps_hbm.at[:, columns], tbuf),
                (values_hbm.at[:, columns], vbuf),
                (fwd_hi_hbm, fwd_hi),
                (fwd_lo_hbm, fwd_lo),
                (inv_hi_hbm, inv_hi),
                (inv_lo_hbm, inv_lo),
                (bias_hbm.at[:, columns], bbuf),
                (gate_hbm, gbuf),
            ]
        )
    ]
    for load in loads:
        load.start()
    loads[0].wait()
    loads[1].wait()

    lower = lax.broadcasted_iota(jnp.int32, (rows, LANES), 1) < HALF
    for tile in range(tiles):
        lanes = slice(tile * LANES, (tile + 1) * LANES)
        value = vbuf[:, lanes].astype(jnp.float32)
        tap = pltpu.roll(tbuf[:, lanes].astype(jnp.float32), HALF, 1)
        packed[2 * tile] = jnp.where(lower, value, tap).astype(jnp.bfloat16)
        packed[2 * tile + 1] = jnp.where(lower, tap, value).astype(jnp.bfloat16)
    blocks[me] = packed[me]

    pl.semaphore_wait(barrier, count - 1)
    sends = []
    for i, offset in enumerate(offsets):
        peer = peer_of(me, offset, count)
        copy = pltpu.make_async_remote_copy(
            src_ref=packed.at[peer],
            dst_ref=blocks.at[me],
            send_sem=send_sem.at[i],
            recv_sem=recv_sem.at[me],
            device_id={"ctx": peer},
            device_id_type=MESH,
        )
        copy.start()
        sends.append(copy)
    for load in loads[2:]:
        load.wait()

    def transform(block):
        data = blocks[block]
        spectrum = jnp.dot(fwd_hi[...], data, preferred_element_type=jnp.float32)
        spectrum = spectrum + jnp.dot(fwd_lo[...], data, preferred_element_type=jnp.float32)
        turned = pltpu.roll(spectrum, HALF, 1)
        spec_a[block] = spectrum
        spec_b[block] = turned
        sum_a[block] = spectrum[:rows] + spectrum[rows:]
        sum_b[block] = turned[:rows] + turned[rows:]

    transform(me)
    for offset in reversed(offsets):
        source = peer_of(me, offset, count)
        pltpu.make_async_remote_copy(
            src_ref=packed.at[source],
            dst_ref=blocks.at[source],
            send_sem=send_sem.at[0],
            recv_sem=recv_sem.at[source],
            device_id={"ctx": source},
            device_id_type=MESH,
        ).wait_recv()
        transform(source)

    group_rows = 8
    sub = lax.broadcasted_iota(jnp.int32, (group_rows, LANES), 0)

    def group(step, carry):
        start = pl.multiple_of(step * group_rows, group_rows)
        real_rows = pl.ds(start, group_rows)
        imag_rows = pl.ds(pl.multiple_of(rows + start, group_rows), group_rows)
        mask = jnp.where(sub + start > 0, 1.0, 0.0)
        sign = jnp.where(step < rows // group_rows // 2, 1.0, -1.0)
        acc = [None] * count
        for a in range(count // 2):
            left = (spec_a[a, real_rows], spec_a[a, imag_rows], sum_a[a, real_rows])
            for b in range(a, count - a):
                right = (spec_b[b, real_rows], spec_b[b, imag_rows], sum_b[b, real_rows])
                if a == b:
                    right = tuple(0.5 * r for r in right)
                terms = tuple(x * y for x, y in zip(left, right))
                old = acc[a + b]
                acc[a + b] = terms if old is None else tuple(x + y for x, y in zip(old, terms))
        before = None
        for n in range(count):
            first, second, third = acc[n]
            now = (first - mask * second, mask * (third - first) - second)
            if before is None:
                mixed = now
            else:
                mixed = (now[0] + sign * before[0], now[1] + sign * before[1])
            total[n, real_rows] = mixed[0]
            total[n, imag_rows] = mixed[1]
            before = now
        return carry

    lax.fori_loop(0, rows // group_rows, group, 0)

    lower_half = lax.broadcasted_iota(jnp.int32, (rows // 2, LANES), 1) < HALF

    def restore(block):
        spectrum = total[block].astype(jnp.bfloat16)
        result = jnp.dot(inv_hi[...], spectrum, preferred_element_type=jnp.float32)
        result = result + jnp.dot(inv_lo[...], spectrum, preferred_element_type=jnp.float32)
        top, bottom = result[: rows // 2], result[rows // 2 :]
        kept = jnp.where(lower_half, top, bottom)
        moved = pltpu.roll(jnp.where(lower_half, bottom, top), HALF, 1)
        return (kept + moved).astype(jnp.bfloat16)

    backs = []
    for i, offset in enumerate(offsets):
        peer = peer_of(me, offset, count)
        ret_send[peer] = restore(peer)
        copy = pltpu.make_async_remote_copy(
            src_ref=ret_send.at[peer],
            dst_ref=ret_recv.at[me],
            send_sem=back_send_sem.at[i],
            recv_sem=back_recv_sem.at[me],
            device_id={"ctx": peer},
            device_id_type=MESH,
        )
        copy.start()
        backs.append(copy)
    ret_recv[me] = restore(me)
    for copy in sends:
        copy.wait_send()
    for offset in reversed(offsets):
        source = peer_of(me, offset, count)
        pltpu.make_async_remote_copy(
            src_ref=ret_send.at[source],
            dst_ref=ret_recv.at[source],
            send_sem=back_send_sem.at[0],
            recv_sem=back_recv_sem.at[source],
            device_id={"ctx": source},
            device_id_type=MESH,
        ).wait_recv()
    for tile in range(tiles):
        lanes = slice(tile * LANES, (tile + 1) * LANES)
        even = ret_recv[2 * tile].astype(jnp.float32)
        odd = ret_recv[2 * tile + 1].astype(jnp.float32)
        top = jnp.where(lower_half, even, pltpu.roll(odd, HALF, 1))
        bottom = jnp.where(lower_half, pltpu.roll(even, HALF, 1), odd)
        skip = bbuf[:, lanes]
        for part, conv in ((slice(0, rows // 2), top), (slice(rows // 2, rows), bottom)):
            value = vbuf[part, lanes].astype(jnp.float32)
            gate = gbuf[part, lanes].astype(jnp.float32)
            out_ref[part, lanes] = (gate * (conv + skip * value)).astype(jnp.bfloat16)
    for copy in backs:
        copy.wait_send()


def solution(mesh):
    count = mesh.shape["ctx"]
    lag_count = mesh.shape["lag"]

    def body(values, gate, bias, filter_taps):
        rows = values.shape[0]
        share = values.shape[1] // lag_count
        (fwd_hi, fwd_lo), (inv_hi, inv_lo) = tables(rows)
        any_spec = pl.BlockSpec(memory_space=pl.ANY)
        bf16, f32 = jnp.bfloat16, jnp.float32
        return pl.pallas_call(
            functools.partial(kernel, count),
            out_shape=jax.ShapeDtypeStruct((rows, share), bf16),
            in_specs=[any_spec] * 8,
            out_specs=pl.BlockSpec(memory_space=pltpu.VMEM),
            scratch_shapes=[
                pltpu.VMEM((rows, share), bf16),
                pltpu.VMEM((rows, share), bf16),
                pltpu.VMEM((rows, share), bf16),
                pltpu.VMEM((1, share), f32),
                pltpu.VMEM((2 * rows, rows), bf16),
                pltpu.VMEM((2 * rows, rows), bf16),
                pltpu.VMEM((rows, 2 * rows), bf16),
                pltpu.VMEM((rows, 2 * rows), bf16),
                pltpu.VMEM((count, rows, LANES), bf16),
                pltpu.VMEM((count, rows, LANES), bf16),
                pltpu.VMEM((count, 2 * rows, LANES), f32),
                pltpu.VMEM((count, rows, LANES), f32),
                pltpu.VMEM((count, 2 * rows, LANES), f32),
                pltpu.VMEM((count, rows, LANES), f32),
                pltpu.VMEM((count, 2 * rows, LANES), f32),
                pltpu.VMEM((count, rows // 2, LANES), bf16),
                pltpu.VMEM((count, rows // 2, LANES), bf16),
                pltpu.SemaphoreType.DMA((8,)),
                pltpu.SemaphoreType.DMA((count,)),
                pltpu.SemaphoreType.DMA((count,)),
                pltpu.SemaphoreType.DMA((count,)),
                pltpu.SemaphoreType.DMA((count,)),
            ],
            compiler_params=pltpu.CompilerParams(collective_id=0, has_side_effects=True),
            name="gated_conv",
        )(
            values,
            filter_taps,
            gate,
            bias.reshape(1, -1),
            jnp.asarray(fwd_hi),
            jnp.asarray(fwd_lo),
            jnp.asarray(inv_hi),
            jnp.asarray(inv_lo),
        )

    return jax.shard_map(
        body,
        mesh=mesh,
        in_specs=(P("ctx", "chan"), P("ctx", ("chan", "lag")), P("chan"), P("ctx", "chan")),
        out_specs=P("ctx", ("chan", "lag")),
        check_vma=False,
    )
```

time: 172 us -> 30 us (0.17); the launches traced: 170 us -> 29.8 us
  local copies, waits for them, and re-layouts: 66.5 us -> 1.67 us
  other arithmetic: 53.1 us -> 0 us
  Pallas kernels: 0 us -> 28.1 us
  waiting for transfers between devices: 13.7 us -> 0 us
  blocking collectives: 13.2 us -> 0 us
  starting transfers between devices: 11.7 us -> 0 us
  matrix products: 11.1 us -> 0 us
    dynamic_slice x100 -> x0, local copies, waits for them, and re-layouts: 63.2 us -> none  [the longest x32 34.9 us: add_lag(): moved_im = lax.dynamic_slice_in_dim(padded_im, start, block_count, 0)]
    add x17 -> x0, other arithmetic: 51.5 us -> none  [the longest x16 51.5 us: add_lag(): acc_im = acc_im + coef_re * moved_im + coef_im * moved_re]
    pallas_call x0 -> x1, Pallas kernels: none -> 28.1 us  [body(): pl.pallas_call(functools.partial(kernel, count), out_shape=jax.ShapeDtype...]
    all_to_all x2 -> x0, waiting for transfers between devices: 13.7 us -> none  [the longest x1 7.58 us: body(): lax.all_to_all(value_share, 'ctx', split_axis=1, concat_axis=0, tiled=True)]
    all_to_all x1 -> x0, blocking collectives: 13.2 us -> none  [body(): lax.all_to_all(before_gate, 'ctx', split_axis=0, concat_axis=1, tiled=True)]
    all_to_all x2 -> x0, starting transfers between devices: 11.7 us -> none  [the longest x1 8.16 us: body(): lax.all_to_all(taps_share, 'ctx', split_axis=1, concat_axis=0, tiled=True)]
    dot_general x14 -> x0, matrix products: 11.1 us -> none  [the longest x3 2.71 us: transform(): jnp.einsum('fm,...mc->...fc', sin_parts[1], operand, preferred_element_ty...]
    concatenate x2 -> x0, local copies, waits for them, and re-layouts: 3.09 us -> none  [the longest x1 1.55 us: body(): padded_re = jnp.concatenate([jnp.zeros_like(val_re), val_re], axis=0)]
  transfers between devices with their start and end apart: 2 -> 0, of which waited for: 2 -> 0; matrix products, arithmetic and copies ran while one was open for 2% -> 0% of each run, Pallas kernels for 0% -> 0%
where the time goes in v1:
time: 30 us; the launch traced here: 29.8 us
  Pallas kernels  28.1 us (94%)
  local copies, waits for them, and re-layouts  1.67 us (6%)
    pallas_call x1, Pallas kernels, body(): pl.pallas_call(functools.partial(kernel, count), out_shape=jax.ShapeDtype...  28.1 us
    unnamed x1, local copies, waits for them, and re-layouts  1.67 us

profile of v1, /device:TPU:0, one launch (start us, length us, event | category | flops | bytes accessed | tf_op | source)
XLA Modules:
  0.0 29.8 jit_solution(15022358880929127342)
XLA Ops:
  0.0 28.1 %gated_conv.1 = bf16[128,1024]{1,0:T(8,128)(2,1)} custom-call(bf16[128,4096]{1,0:T(8,128)(2,1)} %values_hbm.1, bf16[128,4096]{1,0:T(8,128)(2,1)} %taps_hbm.1, bf16[128,1024]{1,0:T(8,128)(2,1)} %gate_hbm.1, f32[1,4096]{1,0:T(1,128)} %bitcast.1, bf16[256,128]{1,0:T(8,128)(2,1)} %constant.8.clone.fwd_hi_hbm, bf16[256,128]{1,0:T(8,128)(2,1)} %constant.9.clone.fwd_lo_hbm, ...), custom_call_target="tpu_custom_call" | custom-call | tf_op jit(solution)/shard_map/gated_conv/pallas_call | solution.py:266
  28.1 1.7 %copy.10 = bf16[128,1024]{1,0:T(8,128)(2,1)} copy(bf16[128,1024]{1,0:T(8,128)(2,1)} %gated_conv.1) | data formatting | bytes 524288

commit v2 on v1

v2 whole, which is shorter than its diff:
```python
import functools
import math

import jax
import jax.numpy as jnp
import numpy as np
from jax import lax
from jax.experimental import pallas as pl
from jax.experimental.pallas import tpu as pltpu
from jax.sharding import PartitionSpec as P

MESH = pl.DeviceIdType.MESH
LANES = 128
HALF = 64
SIDE = 4


def halves(table):
    upper = table.astype(jnp.bfloat16)
    lower = (table - upper.astype(np.float64)).astype(jnp.bfloat16)
    return upper, lower


def tables(rows):
    length = 2 * rows
    order = np.arange(rows)
    freq = np.where(order < rows // 2, 2 * order, 2 * (order - rows // 2) + 1)
    token = np.arange(rows)
    angle = 2.0 * math.pi * ((freq[:, None] * token[None, :]) % length) / length
    alternate = np.where(token % 2 == 0, 1.0, -1.0)
    real, imag = np.cos(angle), -np.sin(angle)
    imag[0] = alternate
    weight = np.where(order == 0, 1.0, 2.0) / length
    back_real = (real * weight[:, None]).T
    back_imag = (imag * weight[:, None]).T
    back_imag[:, 0] = -alternate / length
    forward = np.concatenate([real, imag], axis=0)
    backward = np.concatenate([back_real, back_imag], axis=1)
    return halves(forward), halves(backward)


def hops(offset):
    return sum(min(part, SIDE - part) for part in divmod(offset, SIDE))


def peer_of(me, offset, count):
    dz, dy = divmod(offset, SIDE)
    z, y = me // SIDE, me % SIDE
    return ((z + dz) % (count // SIDE)) * SIDE + (y + dy) % SIDE


def kernel(
    count,
    values_hbm,
    taps_hbm,
    gate_hbm,
    bias_hbm,
    fwd_hbm,
    inv_hbm,
    out_ref,
    vbuf,
    tbuf,
    gbuf,
    bbuf,
    fwd,
    inv,
    packed,
    blocks,
    spec,
    turned,
    last,
    total,
    ret_send,
    ret_recv,
    load_sem,
    send_sem,
    recv_sem,
    back_send_sem,
    back_recv_sem,
):
    me = lax.axis_index("ctx")
    lag = lax.axis_index("lag")
    rows, share = vbuf.shape
    half_rows = rows // 2
    tiles = share // LANES
    middle = count // 2
    offsets = sorted(range(1, count), key=lambda o: -hops(o))

    barrier = pltpu.get_barrier_semaphore()
    for offset in offsets:
        pl.semaphore_signal(
            barrier, inc=1, device_id={"ctx": peer_of(me, offset, count)}, device_id_type=MESH
        )

    columns = pl.ds(pl.multiple_of(lag * share, share), share)
    loads = [
        pltpu.make_async_copy(src, dst, load_sem.at[i])
        for i, (src, dst) in enumerate(
            [
                (taps_hbm.at[:, columns], tbuf),
                (values_hbm.at[:, columns], vbuf),
                (fwd_hbm, fwd),
                (inv_hbm, inv),
                (bias_hbm.at[:, columns], bbuf),
                (gate_hbm, gbuf),
            ]
        )
    ]
    for load in loads:
        load.start()
    loads[0].wait()
    loads[1].wait()

    lower = lax.broadcasted_iota(jnp.int32, (rows, LANES), 1) < HALF
    for tile in range(tiles):
        lanes = slice(tile * LANES, (tile + 1) * LANES)
        value = vbuf[:, lanes].astype(jnp.float32)
        tap = pltpu.roll(tbuf[:, lanes].astype(jnp.float32), HALF, 1)
        packed[2 * tile] = jnp.where(lower, value, tap).astype(jnp.bfloat16)
        packed[2 * tile + 1] = jnp.where(lower, tap, value).astype(jnp.bfloat16)
    blocks[me] = packed[me]
    for load in loads[2:]:
        load.wait()

    pl.semaphore_wait(barrier, count - 1)
    sends = []
    for i, offset in enumerate(offsets):
        peer = peer_of(me, offset, count)
        copy = pltpu.make_async_remote_copy(
            src_ref=packed.at[peer],
            dst_ref=blocks.at[me],
            send_sem=send_sem.at[i],
            recv_sem=recv_sem.at[me],
            device_id={"ctx": peer},
            device_id_type=MESH,
        )
        copy.start()
        sends.append(copy)

    def arrival(buffer, sem, source):
        @pl.when(me != source)
        def _():
            pltpu.make_async_remote_copy(
                src_ref=buffer.at[source],
                dst_ref=buffer.at[source],
                send_sem=send_sem.at[0],
                recv_sem=sem.at[source],
                device_id={"ctx": source},
                device_id_type=MESH,
            ).wait_recv()

    def transform(members):
        for block in members:
            arrival(blocks, recv_sem, block)
        for block in members:
            both = jnp.dot(fwd[...], blocks[block], preferred_element_type=jnp.float32)
            spectrum = both[: 2 * rows] + both[2 * rows :]
            spec[block] = spectrum
            if block < middle:
                turned[block] = pltpu.roll(spectrum, HALF, 1)

    sub = lax.broadcasted_iota(jnp.int32, (8, LANES), 0)

    def products(outputs):
        def group(step, carry):
            sign = jnp.where(step < rows // 32, 1.0, -1.0)
            parts = []
            for part in range(2):
                start = pl.multiple_of(step * 16 + part * 8, 8)
                real_rows = pl.ds(start, 8)
                imag_rows = pl.ds(pl.multiple_of(rows + start, 8), 8)
                mask = jnp.where(sub + start > 0, 1.0, 0.0)

                def triple(ref, block):
                    real, imag = ref[block, real_rows], ref[block, imag_rows]
                    return real, imag, real + imag

                acc = {}
                for a in range(min(middle, outputs.stop // 2 + 1)):
                    left = triple(turned, a)
                    for b in range(max(a, outputs.start - a), outputs.stop - a):
                        right = triple(spec, b)
                        if a == b:
                            right = tuple(0.5 * r for r in right)
                        terms = tuple(x * y for x, y in zip(left, right))
                        old = acc.get(a + b)
                        acc[a + b] = (
                            terms if old is None else tuple(x + y for x, y in zip(old, terms))
                        )
                mixed = []
                before = None
                if outputs.start:
                    before = (last[real_rows], last[imag_rows])
                for n in outputs:
                    first, second, third = acc[n]
                    now = (first - mask * second, mask * (third - first) - second)
                    if before is None:
                        mixed.append(now)
                    else:
                        mixed.append((now[0] + sign * before[0], now[1] + sign * before[1]))
                    before = now
                if outputs.stop < count:
                    last[real_rows] = before[0]
                    last[imag_rows] = before[1]
                parts.append(mixed)
            start = pl.multiple_of(step * 16, 16)
            for n, upper, under in zip(outputs, *parts):
                total[n, pl.ds(start, 16)] = jnp.concatenate(
                    [upper[0], under[0]], axis=0
                ).astype(jnp.bfloat16)
                total[n, pl.ds(pl.multiple_of(rows + start, 16), 16)] = jnp.concatenate(
                    [upper[1], under[1]], axis=0
                ).astype(jnp.bfloat16)
            return carry

        lax.fori_loop(0, rows // 16, group, 0)

    lower_half = lax.broadcasted_iota(jnp.int32, (half_rows, LANES), 1) < HALF

    def restore(block):
        both = jnp.dot(inv[...], total[block], preferred_element_type=jnp.float32)
        result = both[:rows] + both[rows:]
        top, bottom = result[:half_rows], result[half_rows:]
        kept = jnp.where(lower_half, top, bottom)
        moved = pltpu.roll(jnp.where(lower_half, bottom, top), HALF, 1)
        return (kept + moved).astype(jnp.bfloat16)

    def back(block):
        return pltpu.make_async_remote_copy(
            src_ref=ret_send.at[block],
            dst_ref=ret_recv.at[me],
            send_sem=back_send_sem.at[block],
            recv_sem=back_recv_sem.at[me],
            device_id={"ctx": block},
            device_id_type=MESH,
        )

    def finish(outputs):
        width = len(outputs)
        batch = 4
        for first in range(0, width, batch):
            members = [
                outputs.start + (me + first + k) % width for k in range(batch)
            ]
            for block in members:
                ret_send[block] = restore(block)
            for block in members:

                @pl.when(block != me)
                def _():
                    back(block).start()

    quarter = count // 4
    for q in range(4):
        transform(range(q * quarter, (q + 1) * quarter))
        if q == 1:
            products(range(0, middle))
            finish(range(0, middle))
        if q == 3:
            products(range(middle, count))
            finish(range(middle, count))
    ret_recv[me] = ret_send[me]
    for copy in sends:
        copy.wait_send()

    for tile in range(tiles):
        lanes = slice(tile * LANES, (tile + 1) * LANES)
        arrival(ret_recv, back_recv_sem, 2 * tile)
        arrival(ret_recv, back_recv_sem, 2 * tile + 1)
        even = ret_recv[2 * tile].astype(jnp.float32)
        odd = ret_recv[2 * tile + 1].astype(jnp.float32)
        top = jnp.where(lower_half, even, pltpu.roll(odd, HALF, 1))
        bottom = jnp.where(lower_half, pltpu.roll(even, HALF, 1), odd)
        skip = bbuf[:, lanes]
        for part, conv in ((slice(0, half_rows), top), (slice(half_rows, rows), bottom)):
            value = vbuf[part, lanes].astype(jnp.float32)
            gate = gbuf[part, lanes].astype(jnp.float32)
            out_ref[part, lanes] = (gate * (conv + skip * value)).astype(jnp.bfloat16)
    for block in range(count):

        @pl.when(block != me)
        def _():
            back(block).wait_send()


def solution(mesh):
    count = mesh.shape["ctx"]
    lag_count = mesh.shape["lag"]

    def body(values, gate, bias, filter_taps):
        rows = values.shape[0]
        share = values.shape[1] // lag_count
        forward, inverse = tables(rows)
        any_spec = pl.BlockSpec(memory_space=pltpu.HBM)
        bf16, f32 = jnp.bfloat16, jnp.float32
        return pl.pallas_call(
            functools.partial(kernel, count),
            out_shape=pltpu.VMEM((rows, share), bf16),
            in_specs=[any_spec] * 6,
            out_specs=pl.BlockSpec(memory_space=pltpu.VMEM),
            scratch_shapes=[
                pltpu.VMEM((rows, share), bf16),
                pltpu.VMEM((rows, share), bf16),
                pltpu.VMEM((rows, share), bf16),
                pltpu.VMEM((1, share), f32),
                pltpu.VMEM((4 * rows, rows), bf16),
                pltpu.VMEM((2 * rows, 2 * rows), bf16),
                pltpu.VMEM((count, rows, LANES), bf16),
                pltpu.VMEM((count, rows, LANES), bf16),
                pltpu.VMEM((count, 2 * rows, LANES), f32),
                pltpu.VMEM((count // 2, 2 * rows, LANES), f32),
                pltpu.VMEM((2 * rows, LANES), f32),
                pltpu.VMEM((count, 2 * rows, LANES), bf16),
                pltpu.VMEM((count, rows // 2, LANES), bf16),
                pltpu.VMEM((count, rows // 2, LANES), bf16),
                pltpu.SemaphoreType.DMA((6,)),
                pltpu.SemaphoreType.DMA((count,)),
                pltpu.SemaphoreType.DMA((count,)),
                pltpu.SemaphoreType.DMA((count,)),
                pltpu.SemaphoreType.DMA((count,)),
            ],
            compiler_params=pltpu.CompilerParams(
                collective_id=0, has_side_effects=True, vmem_limit_bytes=60 * 2**20
            ),
            name="gated_conv",
        )(
            values,
            filter_taps,
            gate,
            bias.reshape(1, -1),
            jnp.asarray(np.concatenate(forward, axis=0)),
            jnp.asarray(np.concatenate(inverse, axis=0)),
        )

    return jax.shard_map(
        body,
        mesh=mesh,
        in_specs=(P("ctx", "chan"), P("ctx", ("chan", "lag")), P("chan"), P("ctx", "chan")),
        out_specs=P("ctx", ("chan", "lag")),
        check_vma=False,
    )
```

time: 30 us -> 23.2 us (0.77)
  Pallas kernels: 28.1 us -> 22.1 us
  local copies, waits for them, and re-layouts: 1.67 us -> 0.71 us
    pallas_call x1, Pallas kernels: 28.1 us -> 22.1 us  [body(): pl.pallas_call(functools.partial(kernel, count), out_shape=pltpu.VMEM((ro...]
    unnamed x1, local copies, waits for them, and re-layouts: 1.67 us -> 0.71 us
where the time goes in v2:
time: 23.2 us; the launch traced here: 22.8 us
  Pallas kernels  22.1 us (95%)
  local copies, waits for them, and re-layouts  0.71 us (3%)
    pallas_call x1, Pallas kernels, body(): pl.pallas_call(functools.partial(kernel, count), out_shape=pltpu.VMEM((ro...  22.1 us
    unnamed x1, local copies, waits for them, and re-layouts  0.71 us

profile of v2, /device:TPU:0, one launch (start us, length us, event | category | flops | bytes accessed | tf_op | source)
XLA Modules:
  0.0 22.8 jit_solution(12128301945429482680)
XLA Ops:
  0.0 22.1 %gated_conv.1 = bf16[128,1024]{1,0:T(8,128)(2,1)S(1)} custom-call(bf16[128,4096]{1,0:T(8,128)(2,1)} %values_hbm.1, bf16[128,4096]{1,0:T(8,128)(2,1)} %taps_hbm.1, bf16[128,1024]{1,0:T(8,128)(2,1)} %gate_hbm.1, f32[1,4096]{1,0:T(1,128)} %bitcast.1, bf16[512,128]{1,0:T(8,128)(2,1)} %constant.4.clone.fwd_hbm, bf16[256,256]{1,0:T(8,128)(2,1)} %constant.5.clone.inv_hbm), custom_call_target="tpu_custom_call" | custom-call | tf_op jit(solution)/shard_map/gated_conv/pallas_call | solution.py:296
  22.1 0.7 %copy.8 = bf16[128,1024]{1,0:T(8,128)(2,1)} copy(bf16[128,1024]{1,0:T(8,128)(2,1)S(1)} %gated_conv.1) | data formatting | bytes 524288

commit v3 on v2

--- a/solution.py
+++ b/solution.py
@@ -39,14 +39,14 @@
     return halves(forward), halves(backward)
 
 
-def hops(offset):
-    return sum(min(part, SIDE - part) for part in divmod(offset, SIDE))
+OFFSETS = (6, 9, 14, 11, 10, 5, 15, 7, 13, 2, 8, 1, 4, 3, 12)
 
 
 def peer_of(me, offset, count):
     dz, dy = divmod(offset, SIDE)
-    z, y = me // SIDE, me % SIDE
-    return ((z + dz) % (count // SIDE)) * SIDE + (y + dy) % SIDE
+    row = (me + dz * SIDE) & (count - SIDE) if dz else me & (count - SIDE)
+    column = (me + dy) & (SIDE - 1) if dy else me & (SIDE - 1)
+    return row + column
 
 
 def kernel(
@@ -69,6 +69,7 @@
     spec,
     turned,
     last,
+    partial,
     total,
     ret_send,
     ret_recv,
@@ -84,13 +85,8 @@
     half_rows = rows // 2
     tiles = share // LANES
     middle = count // 2
-    offsets = sorted(range(1, count), key=lambda o: -hops(o))
-
-    barrier = pltpu.get_barrier_semaphore()
-    for offset in offsets:
-        pl.semaphore_signal(
-            barrier, inc=1, device_id={"ctx": peer_of(me, offset, count)}, device_id_type=MESH
-        )
+    quarter = count // 4
+    offsets = list(OFFSETS)
 
     columns = pl.ds(pl.multiple_of(lag * share, share), share)
     loads = [
@@ -106,7 +102,14 @@
             ]
         )
     ]
-    for load in loads:
+    for load in loads[:2]:
+        load.start()
+    barrier = pltpu.get_barrier_semaphore()
+    for offset in offsets:
+        pl.semaphore_signal(
+            barrier, inc=1, device_id={"ctx": peer_of(me, offset, count)}, device_id_type=MESH
+        )
+    for load in loads[2:]:
         load.start()
     loads[0].wait()
     loads[1].wait()
@@ -161,7 +164,14 @@
 
     sub = lax.broadcasted_iota(jnp.int32, (8, LANES), 0)
 
-    def products(outputs):
+    def products(stage):
+        members = range(stage * quarter, (stage + 1) * quarter)
+        pairs = [(a, b) for b in members for a in range(min(b, count - 1 - b) + 1)]
+        touched = sorted({a + b for a, b in pairs} | set(members))
+        began = {
+            a + b for b in range(members.start) for a in range(min(b, count - 1 - b) + 1)
+        }
+
         def group(step, carry):
             sign = jnp.where(step < rows // 32, 1.0, -1.0)
             parts = []
@@ -176,22 +186,28 @@
                     return real, imag, real + imag
 
                 acc = {}
-                for a in range(min(middle, outputs.stop // 2 + 1)):
+                for n in touched:
+                    if n in began:
+                        acc[n] = tuple(partial[n, k, real_rows] for k in range(3))
+                right = {b: triple(spec, b) for b in members}
+                for a in range(max(a for a, _ in pairs) + 1):
                     left = triple(turned, a)
-                    for b in range(max(a, outputs.start - a), outputs.stop - a):
-                        right = triple(spec, b)
-                        if a == b:
-                            right = tuple(0.5 * r for r in right)
-                        terms = tuple(x * y for x, y in zip(left, right))
+                    for b in members:
+                        if (a, b) not in pairs:
+                            continue
+                        other = right[b] if a != b else tuple(0.5 * r for r in right[b])
+                        terms = tuple(x * y for x, y in zip(left, other))
                         old = acc.get(a + b)
                         acc[a + b] = (
                             terms if old is None else tuple(x + y for x, y in zip(old, terms))
                         )
+                for n in touched:
+                    if n >= members.stop:
+                        for k in range(3):
+                            partial[n, k, real_rows] = acc[n][k]
                 mixed = []
-                before = None
-                if outputs.start:
-                    before = (last[real_rows], last[imag_rows])
-                for n in outputs:
+                before = (last[real_rows], last[imag_rows]) if stage else None
+                for n in members:
                     first, second, third = acc[n]
                     now = (first - mask * second, mask * (third - first) - second)
                     if before is None:
@@ -199,12 +215,12 @@
                     else:
                         mixed.append((now[0] + sign * before[0], now[1] + sign * before[1]))
                     before = now
-                if outputs.stop < count:
+                if members.stop < count:
                     last[real_rows] = before[0]
                     last[imag_rows] = before[1]
                 parts.append(mixed)
             start = pl.multiple_of(step * 16, 16)
-            for n, upper, under in zip(outputs, *parts):
+            for n, upper, under in zip(members, *parts):
                 total[n, pl.ds(start, 16)] = jnp.concatenate(
                     [upper[0], under[0]], axis=0
                 ).astype(jnp.bfloat16)
@@ -213,7 +229,7 @@
                 ).astype(jnp.bfloat16)
             return carry
 
-        lax.fori_loop(0, rows // 16, group, 0)
+        lax.fori_loop(0, rows // 16, group, 0, unroll=True)
 
     lower_half = lax.broadcasted_iota(jnp.int32, (half_rows, LANES), 1) < HALF
 
@@ -235,30 +251,20 @@
             device_id_type=MESH,
         )
 
-    def finish(outputs):
-        width = len(outputs)
-        batch = 4
-        for first in range(0, width, batch):
-            members = [
-                outputs.start + (me + first + k) % width for k in range(batch)
-            ]
-            for block in members:
-                ret_send[block] = restore(block)
-            for block in members:
-
-                @pl.when(block != me)
-                def _():
-                    back(block).start()
-
-    quarter = count // 4
-    for q in range(4):
-        transform(range(q * quarter, (q + 1) * quarter))
-        if q == 1:
-            products(range(0, middle))
-            finish(range(0, middle))
-        if q == 3:
-            products(range(middle, count))
-            finish(range(middle, count))
+    def finish(stage):
+        members = [stage * quarter + ((me + k) & (quarter - 1)) for k in range(quarter)]
+        for block in members:
+            ret_send[block] = restore(block)
+        for block in members:
+
+            @pl.when(block != me)
+            def _():
+                back(block).start()
+
+    for stage in range(4):
+        transform(range(stage * quarter, (stage + 1) * quarter))
+        products(stage)
+        finish(stage)
     ret_recv[me] = ret_send[me]
     for copy in sends:
         copy.wait_send()
@@ -310,6 +316,7 @@
                 pltpu.VMEM((count, 2 * rows, LANES), f32),
                 pltpu.VMEM((count // 2, 2 * rows, LANES), f32),
                 pltpu.VMEM((2 * rows, LANES), f32),
+                pltpu.VMEM((count, 3, rows, LANES), f32),
                 pltpu.VMEM((count, 2 * rows, LANES), bf16),
                 pltpu.VMEM((count, rows // 2, LANES), bf16),
                 pltpu.VMEM((count, rows // 2, LANES), bf16),

time: 23.2 us -> 22.5 us (0.970)
  the two profiles are of different devices: /device:TPU:0 before, /device:TPU:100 now
where the time goes in v3:
time: 22.5 us; the launch traced here: 22.4 us
  Pallas kernels  21.7 us (96%)
  local copies, waits for them, and re-layouts  0.71 us (3%)
    pallas_call x1, Pallas kernels, body(): pl.pallas_call(functools.partial(kernel, count), out_shape=pltpu.VMEM((ro...  21.7 us
    unnamed x1, local copies, waits for them, and re-layouts  0.71 us

profile of v3, /device:TPU:100, one launch (start us, length us, event | category | flops | bytes accessed | tf_op | source)
XLA Modules:
  0.0 22.4 jit_solution(12377550708750247235)
XLA Ops:
  0.0 21.7 %gated_conv.1 = bf16[128,1024]{1,0:T(8,128)(2,1)S(1)} custom-call(bf16[128,4096]{1,0:T(8,128)(2,1)} %values_hbm.1, bf16[128,4096]{1,0:T(8,128)(2,1)} %taps_hbm.1, bf16[128,1024]{1,0:T(8,128)(2,1)} %gate_hbm.1, f32[1,4096]{1,0:T(1,128)} %bitcast.1, bf16[512,128]{1,0:T(8,128)(2,1)} %constant.4.clone.fwd_hbm, bf16[256,256]{1,0:T(8,128)(2,1)} %constant.5.clone.inv_hbm), custom_call_target="tpu_custom_call" | custom-call | tf_op jit(solution)/shard_map/gated_conv/pallas_call | solution.py:302
  21.7 0.7 %copy.8 = bf16[128,1024]{1,0:T(8,128)(2,1)} copy(bf16[128,1024]{1,0:T(8,128)(2,1)S(1)} %gated_conv.1) | data formatting | bytes 524288

commit v4 on v3

--- a/solution.py
+++ b/solution.py
@@ -12,7 +12,6 @@
 MESH = pl.DeviceIdType.MESH
 LANES = 128
 HALF = 64
-SIDE = 4
 
 
 def halves(table):
@@ -39,14 +38,7 @@
     return halves(forward), halves(backward)
 
 
-OFFSETS = (6, 9, 14, 11, 10, 5, 15, 7, 13, 2, 8, 1, 4, 3, 12)
-
-
-def peer_of(me, offset, count):
-    dz, dy = divmod(offset, SIDE)
-    row = (me + dz * SIDE) & (count - SIDE) if dz else me & (count - SIDE)
-    column = (me + dy) & (SIDE - 1) if dy else me & (SIDE - 1)
-    return row + column
+MASKS = (10, 6, 9, 14, 11, 8, 2, 5, 15, 7, 13, 1, 4, 3, 12)
 
 
 def kernel(
@@ -86,7 +78,7 @@
     tiles = share // LANES
     middle = count // 2
     quarter = count // 4
-    offsets = list(OFFSETS)
+    peers = [me ^ mask for mask in MASKS]
 
     columns = pl.ds(pl.multiple_of(lag * share, share), share)
     loads = [
@@ -105,10 +97,8 @@
     for load in loads[:2]:
         load.start()
     barrier = pltpu.get_barrier_semaphore()
-    for offset in offsets:
-        pl.semaphore_signal(
-            barrier, inc=1, device_id={"ctx": peer_of(me, offset, count)}, device_id_type=MESH
-        )
+    for peer in peers:
+        pl.semaphore_signal(barrier, inc=1, device_id={"ctx": peer}, device_id_type=MESH)
     for load in loads[2:]:
         load.start()
     loads[0].wait()
@@ -126,19 +116,19 @@
         load.wait()
 
     pl.semaphore_wait(barrier, count - 1)
-    sends = []
-    for i, offset in enumerate(offsets):
-        peer = peer_of(me, offset, count)
-        copy = pltpu.make_async_remote_copy(
+
+    def send(peer):
+        return pltpu.make_async_remote_copy(
             src_ref=packed.at[peer],
             dst_ref=blocks.at[me],
-            send_sem=send_sem.at[i],
+            send_sem=send_sem.at[peer],
             recv_sem=recv_sem.at[me],
             device_id={"ctx": peer},
             device_id_type=MESH,
         )
-        copy.start()
-        sends.append(copy)
+
+    for peer in peers:
+        send(peer).start()
 
     def arrival(buffer, sem, source):
         @pl.when(me != source)
@@ -152,25 +142,34 @@
                 device_id_type=MESH,
             ).wait_recv()
 
-    def transform(members):
+    def row_blocks(row):
+        return range(row * quarter, (row + 1) * quarter)
+
+    def transform(row):
+        members = row_blocks(row)
         for block in members:
             arrival(blocks, recv_sem, block)
-        for block in members:
-            both = jnp.dot(fwd[...], blocks[block], preferred_element_type=jnp.float32)
-            spectrum = both[: 2 * rows] + both[2 * rows :]
-            spec[block] = spectrum
-            if block < middle:
-                turned[block] = pltpu.roll(spectrum, HALF, 1)
+        for block in members[::2]:
+            pair = jnp.concatenate([blocks[block], blocks[block + 1]], axis=1)
+            both = jnp.dot(fwd[...], pair, preferred_element_type=jnp.float32)
+            spectra = both[: 2 * rows] + both[2 * rows :]
+            for k in range(2):
+                spectrum = spectra[:, k * LANES : (k + 1) * LANES]
+                spec[block + k] = spectrum
+                if block < middle:
+                    turned[block + k] = pltpu.roll(spectrum, HALF, 1)
 
     sub = lax.broadcasted_iota(jnp.int32, (8, LANES), 0)
 
-    def products(stage):
-        members = range(stage * quarter, (stage + 1) * quarter)
-        pairs = [(a, b) for b in members for a in range(min(b, count - 1 - b) + 1)]
-        touched = sorted({a + b for a, b in pairs} | set(members))
-        began = {
-            a + b for b in range(members.start) for a in range(min(b, count - 1 - b) + 1)
-        }
+    begun, closed = set(), []
+
+    def products(pairs, close):
+        closing = [n for row in close for n in range(row * quarter, (row + 1) * quarter)]
+        touched = sorted({a + b for a, b in pairs} | set(closing))
+        loaded = [n for n in touched if n in begun]
+        first_close = not closed
+        lefts = sorted({a for a, _ in pairs})
+        rights = sorted({b for _, b in pairs})
 
         def group(step, carry):
             sign = jnp.where(step < rows // 32, 1.0, -1.0)
@@ -186,13 +185,12 @@
                     return real, imag, real + imag
 
                 acc = {}
-                for n in touched:
-                    if n in began:
-                        acc[n] = tuple(partial[n, k, real_rows] for k in range(3))
-                right = {b: triple(spec, b) for b in members}
-                for a in range(max(a for a, _ in pairs) + 1):
+                for n in loaded:
+                    acc[n] = tuple(partial[n, k, real_rows] for k in range(3))
+                right = {b: triple(spec, b) for b in rights}
+                for a in lefts:
                     left = triple(turned, a)
-                    for b in members:
+                    for b in rights:
                         if (a, b) not in pairs:
                             continue
                         other = right[b] if a != b else tuple(0.5 * r for r in right[b])
@@ -202,12 +200,14 @@
                             terms if old is None else tuple(x + y for x, y in zip(old, terms))
                         )
                 for n in touched:
-                    if n >= members.stop:
+                    if n not in closing:
                         for k in range(3):
                             partial[n, k, real_rows] = acc[n][k]
+                if not closing:
+                    continue
                 mixed = []
-                before = (last[real_rows], last[imag_rows]) if stage else None
-                for n in members:
+                before = None if first_close else (last[real_rows], last[imag_rows])
+                for n in closing:
                     first, second, third = acc[n]
                     now = (first - mask * second, mask * (third - first) - second)
                     if before is None:
@@ -215,12 +215,14 @@
                     else:
                         mixed.append((now[0] + sign * before[0], now[1] + sign * before[1]))
                     before = now
-                if members.stop < count:
+                if closing[-1] < count - 1:
                     last[real_rows] = before[0]
                     last[imag_rows] = before[1]
                 parts.append(mixed)
+            if not closing:
+                return carry
             start = pl.multiple_of(step * 16, 16)
-            for n, upper, under in zip(members, *parts):
+            for n, upper, under in zip(closing, *parts):
                 total[n, pl.ds(start, 16)] = jnp.concatenate(
                     [upper[0], under[0]], axis=0
                 ).astype(jnp.bfloat16)
@@ -230,16 +232,21 @@
             return carry
 
         lax.fori_loop(0, rows // 16, group, 0, unroll=True)
+        begun.update(touched)
+        closed.extend(closing)
 
     lower_half = lax.broadcasted_iota(jnp.int32, (half_rows, LANES), 1) < HALF
 
-    def restore(block):
-        both = jnp.dot(inv[...], total[block], preferred_element_type=jnp.float32)
-        result = both[:rows] + both[rows:]
-        top, bottom = result[:half_rows], result[half_rows:]
-        kept = jnp.where(lower_half, top, bottom)
-        moved = pltpu.roll(jnp.where(lower_half, bottom, top), HALF, 1)
-        return (kept + moved).astype(jnp.bfloat16)
+    def restore(first, second):
+        pair = jnp.concatenate([total[first], total[second]], axis=1)
+        both = jnp.dot(inv[...], pair, preferred_element_type=jnp.float32)
+        results = both[:rows] + both[rows:]
+        for k, block in enumerate((first, second)):
+            result = results[:, k * LANES : (k + 1) * LANES]
+            top, bottom = result[:half_rows], result[half_rows:]
+            kept = jnp.where(lower_half, top, bottom)
+            moved = pltpu.roll(jnp.where(lower_half, bottom, top), HALF, 1)
+            ret_send[block] = (kept + moved).astype(jnp.bfloat16)
 
     def back(block):
         return pltpu.make_async_remote_copy(
@@ -251,23 +258,40 @@
             device_id_type=MESH,
         )
 
-    def finish(stage):
-        members = [stage * quarter + ((me + k) & (quarter - 1)) for k in range(quarter)]
-        for block in members:
-            ret_send[block] = restore(block)
-        for block in members:
-
-            @pl.when(block != me)
-            def _():
-                back(block).start()
-
-    for stage in range(4):
-        transform(range(stage * quarter, (stage + 1) * quarter))
-        products(stage)
-        finish(stage)
+    def finish(*groups):
+        for members in groups:
+            for first, second in zip(members[::2], members[1::2]):
+                restore(first, second)
+            for block in members:
+
+                @pl.when(block != me)
+                def _():
+                    back(block).start()
+
+    def pairs_of(left, right):
+        return [
+            (a, b)
+            for a in row_blocks(left)
+            for b in row_blocks(right)
+            if a <= b and a + b < count
+        ]
+
+    transform(3)
+    transform(2)
+    transform(0)
+    products(pairs_of(0, 0), [0])
+    finish([0, 1, 3, 2])
+    products(pairs_of(0, 2) + pairs_of(0, 3), [])
+    transform(1)
+    products(pairs_of(0, 1) + pairs_of(1, 1), [1])
+    finish([4, 5, 7, 6])
+    products(pairs_of(1, 2), [2])
+    finish([8, 9, 11, 10])
+    products([], [3])
+    finish([12, 13, 15, 14])
     ret_recv[me] = ret_send[me]
-    for copy in sends:
-        copy.wait_send()
+    for peer in peers:
+        send(peer).wait_send()
 
     for tile in range(tiles):
         lanes = slice(tile * LANES, (tile + 1) * LANES)

time: 22.5 us -> 21.8 us (0.969)
  the two profiles are of different devices: /device:TPU:100 before, /device:TPU:0 now
where the time goes in v4:
time: 21.8 us; the launch traced here: 21.6 us
  Pallas kernels  20.8 us (95%)
  local copies, waits for them, and re-layouts  0.71 us (3%)
    pallas_call x1, Pallas kernels, body(): pl.pallas_call(functools.partial(kernel, count), out_shape=pltpu.VMEM((ro...  20.8 us
    unnamed x1, local copies, waits for them, and re-layouts  0.71 us

profile of v4, /device:TPU:0, one launch (start us, length us, event | category | flops | bytes accessed | tf_op | source)
XLA Modules:
  0.0 21.6 jit_solution(4212079067392925746)
XLA Ops:
  0.0 20.8 %gated_conv.1 = bf16[128,1024]{1,0:T(8,128)(2,1)S(1)} custom-call(bf16[128,4096]{1,0:T(8,128)(2,1)} %values_hbm.1, bf16[128,4096]{1,0:T(8,128)(2,1)} %taps_hbm.1, bf16[128,1024]{1,0:T(8,128)(2,1)} %gate_hbm.1, f32[1,4096]{1,0:T(1,128)} %bitcast.1, bf16[512,128]{1,0:T(8,128)(2,1)} %constant.4.clone.fwd_hbm, bf16[256,256]{1,0:T(8,128)(2,1)} %constant.5.clone.inv_hbm), custom_call_target="tpu_custom_call" | custom-call | tf_op jit(solution)/shard_map/gated_conv/pallas_call | solution.py:326
  20.8 0.7 %copy.8 = bf16[128,1024]{1,0:T(8,128)(2,1)} copy(bf16[128,1024]{1,0:T(8,128)(2,1)S(1)} %gated_conv.1) | data formatting | bytes 524288

commit v5 on v4

--- a/solution.py
+++ b/solution.py
@@ -80,6 +80,10 @@
     quarter = count // 4
     peers = [me ^ mask for mask in MASKS]
 
+    barrier = pltpu.get_barrier_semaphore()
+    for peer in peers:
+        pl.semaphore_signal(barrier, inc=1, device_id={"ctx": peer}, device_id_type=MESH)
+
     columns = pl.ds(pl.multiple_of(lag * share, share), share)
     loads = [
         pltpu.make_async_copy(src, dst, load_sem.at[i])
@@ -96,9 +100,6 @@
     ]
     for load in loads[:2]:
         load.start()
-    barrier = pltpu.get_barrier_semaphore()
-    for peer in peers:
-        pl.semaphore_signal(barrier, inc=1, device_id={"ctx": peer}, device_id_type=MESH)
     for load in loads[2:]:
         load.start()
     loads[0].wait()
@@ -240,7 +241,7 @@
     def restore(first, second):
         pair = jnp.concatenate([total[first], total[second]], axis=1)
         both = jnp.dot(inv[...], pair, preferred_element_type=jnp.float32)
-        results = both[:rows] + both[rows:]
+        results = both
         for k, block in enumerate((first, second)):
             result = results[:, k * LANES : (k + 1) * LANES]
             top, bottom = result[:half_rows], result[half_rows:]
@@ -280,15 +281,15 @@
     transform(2)
     transform(0)
     products(pairs_of(0, 0), [0])
-    finish([0, 1, 3, 2])
+    finish([0, 1])
     products(pairs_of(0, 2) + pairs_of(0, 3), [])
     transform(1)
     products(pairs_of(0, 1) + pairs_of(1, 1), [1])
-    finish([4, 5, 7, 6])
+    finish([4, 5, 3, 2])
     products(pairs_of(1, 2), [2])
-    finish([8, 9, 11, 10])
+    finish([8, 9, 7, 6])
     products([], [3])
-    finish([12, 13, 15, 14])
+    finish([12, 13, 11, 10], [15, 14])
     ret_recv[me] = ret_send[me]
     for peer in peers:
         send(peer).wait_send()
@@ -334,7 +335,7 @@
                 pltpu.VMEM((rows, share), bf16),
                 pltpu.VMEM((1, share), f32),
                 pltpu.VMEM((4 * rows, rows), bf16),
-                pltpu.VMEM((2 * rows, 2 * rows), bf16),
+                pltpu.VMEM((rows, 2 * rows), bf16),
                 pltpu.VMEM((count, rows, LANES), bf16),
                 pltpu.VMEM((count, rows, LANES), bf16),
                 pltpu.VMEM((count, 2 * rows, LANES), f32),
@@ -360,7 +361,7 @@
             gate,
             bias.reshape(1, -1),
             jnp.asarray(np.concatenate(forward, axis=0)),
-            jnp.asarray(np.concatenate(inverse, axis=0)),
+            jnp.asarray(inverse[0]),
         )
 
     return jax.shard_map(

time: 21.8 us -> 21.6 us (level)
  no operation moved by 1% of the time
where the time goes in v5:
time: 21.6 us; the launch traced here: 21.4 us
  Pallas kernels  20.7 us (96%)
  local copies, waits for them, and re-layouts  0.71 us (3%)
    pallas_call x1, Pallas kernels, body(): pl.pallas_call(functools.partial(kernel, count), out_shape=pltpu.VMEM((ro...  20.7 us
    unnamed x1, local copies, waits for them, and re-layouts  0.71 us

profile of v5, /device:TPU:0, one launch (start us, length us, event | category | flops | bytes accessed | tf_op | source)
XLA Modules:
  0.0 21.4 jit_solution(15032139842316559113)
XLA Ops:
  0.0 20.7 %gated_conv.1 = bf16[128,1024]{1,0:T(8,128)(2,1)S(1)} custom-call(bf16[128,4096]{1,0:T(8,128)(2,1)} %values_hbm.1, bf16[128,4096]{1,0:T(8,128)(2,1)} %taps_hbm.1, bf16[128,1024]{1,0:T(8,128)(2,1)} %gate_hbm.1, f32[1,4096]{1,0:T(1,128)} %bitcast.1, bf16[512,128]{1,0:T(8,128)(2,1)} %constant.4.clone.fwd_hbm, bf16[128,256]{1,0:T(8,128)(2,1)} %constant.5.clone.inv_hbm), custom_call_target="tpu_custom_call" | custom-call | tf_op jit(solution)/shard_map/gated_conv/pallas_call | solution.py:327
  20.7 0.7 %copy.8 = bf16[128,1024]{1,0:T(8,128)(2,1)} copy(bf16[128,1024]{1,0:T(8,128)(2,1)S(1)} %gated_conv.1) | data formatting | bytes 524288

commit v6 on v5

--- a/solution.py
+++ b/solution.py
@@ -294,8 +294,9 @@
     for peer in peers:
         send(peer).wait_send()
 
-    for tile in range(tiles):
-        lanes = slice(tile * LANES, (tile + 1) * LANES)
+    for step in (0, 2, 1, 6, 3, 4, 7, 5):
+        tile = (me // 2) ^ step
+        lanes = pl.ds(pl.multiple_of(tile * LANES, LANES), LANES)
         arrival(ret_recv, back_recv_sem, 2 * tile)
         arrival(ret_recv, back_recv_sem, 2 * tile + 1)
         even = ret_recv[2 * tile].astype(jnp.float32)

time: 21.6 us -> 21.6 us (level)
  no operation moved by 1% of the time
where the time goes in v6:
time: 21.6 us; the launch traced here: 21.5 us
  Pallas kernels  20.8 us (96%)
  local copies, waits for them, and re-layouts  0.71 us (3%)
    pallas_call x1, Pallas kernels, body(): pl.pallas_call(functools.partial(kernel, count), out_shape=pltpu.VMEM((ro...  20.8 us
    unnamed x1, local copies, waits for them, and re-layouts  0.71 us

profile of v6, /device:TPU:0, one launch (start us, length us, event | category | flops | bytes accessed | tf_op | source)
XLA Modules:
  0.0 21.5 jit_solution(8690297096209976472)
XLA Ops:
  0.0 20.8 %gated_conv.1 = bf16[128,1024]{1,0:T(8,128)(2,1)S(1)} custom-call(bf16[128,4096]{1,0:T(8,128)(2,1)} %values_hbm.1, bf16[128,4096]{1,0:T(8,128)(2,1)} %taps_hbm.1, bf16[128,1024]{1,0:T(8,128)(2,1)} %gate_hbm.1, f32[1,4096]{1,0:T(1,128)} %bitcast.1, bf16[512,128]{1,0:T(8,128)(2,1)} %constant.4.clone.fwd_hbm, bf16[128,256]{1,0:T(8,128)(2,1)} %constant.5.clone.inv_hbm), custom_call_target="tpu_custom_call" | custom-call | tf_op jit(solution)/shard_map/gated_conv/pallas_call | solution.py:328
  20.8 0.7 %copy.8 = bf16[128,1024]{1,0:T(8,128)(2,1)} copy(bf16[128,1024]{1,0:T(8,128)(2,1)S(1)} %gated_conv.1) | data formatting | bytes 524288

commit v7 on v5

--- a/solution.py
+++ b/solution.py
@@ -38,7 +38,7 @@
     return halves(forward), halves(backward)
 
 
-MASKS = (10, 6, 9, 14, 11, 8, 2, 5, 15, 7, 13, 1, 4, 3, 12)
+MASKS = (10, 14, 6, 11, 9, 8, 2, 15, 5, 13, 7, 12, 4, 3, 1)
 
 
 def kernel(

time: 21.6 us -> 21.7 us (level)
  no operation moved by 1% of the time
where the time goes in v7:
time: 21.7 us; the launch traced here: 21.5 us
  Pallas kernels  20.8 us (96%)
  local copies, waits for them, and re-layouts  0.71 us (3%)
    pallas_call x1, Pallas kernels, body(): pl.pallas_call(functools.partial(kernel, count), out_shape=pltpu.VMEM((ro...  20.8 us
    unnamed x1, local copies, waits for them, and re-layouts  0.71 us

profile of v7, /device:TPU:0, one launch (start us, length us, event | category | flops | bytes accessed | tf_op | source)
XLA Modules:
  0.0 21.5 jit_solution(4674090757050819909)
XLA Ops:
  0.0 20.8 %gated_conv.1 = bf16[128,1024]{1,0:T(8,128)(2,1)S(1)} custom-call(bf16[128,4096]{1,0:T(8,128)(2,1)} %values_hbm.1, bf16[128,4096]{1,0:T(8,128)(2,1)} %taps_hbm.1, bf16[128,1024]{1,0:T(8,128)(2,1)} %gate_hbm.1, f32[1,4096]{1,0:T(1,128)} %bitcast.1, bf16[512,128]{1,0:T(8,128)(2,1)} %constant.4.clone.fwd_hbm, bf16[128,256]{1,0:T(8,128)(2,1)} %constant.5.clone.inv_hbm), custom_call_target="tpu_custom_call" | custom-call | tf_op jit(solution)/shard_map/gated_conv/pallas_call | solution.py:327
  20.8 0.7 %copy.8 = bf16[128,1024]{1,0:T(8,128)(2,1)} copy(bf16[128,1024]{1,0:T(8,128)(2,1)S(1)} %gated_conv.1) | data formatting | bytes 524288
